TPU v7x, 256 devices: a whole 4x4x8 slice. The times are simulated.
256 devices in a mesh: box: 16 (over x_lo, y, core), samp: 16 (over z, x_hi).
Axes of the slice: x: 4 (x_hi: 2, x_lo: 2; x = x_hi * 2 + x_lo), y: 4, z: 8, core: 2. Of those that a mesh axis runs over, the one named last changes fastest.
Arguments:
- xvec: bfloat16 [4096, 2, 4, 128], P(('box', 'samp')), may hold values from -6 to 6
- near_blocks: bfloat16 [4096, 8, 2, 128, 128], P(('box', 'samp')), may hold values from -0.1875 to 0.1875
- neighbours: int32 [4096, 8], P(('box', 'samp')), may hold values from 0 to 4095, as said below
- lift: bfloat16 [4096, 2, 128, 128], P(('box', 'samp')), may hold values from -0.5 to 0.5
- place: bfloat16 [4096, 2, 128, 128], P(('box', 'samp')), may hold values from -0.25 to 0.25
- interp: bfloat16 [2048, 128], replicated, may hold values from -0.5 to 0.5
- phases: float32 [8, 2, 2048], replicated, may hold values from -1 to 1, as said below
- octant: int32 [4096], P(('box', 'samp')), may hold values from 0 to 7, as said below
- leaf_parent_index: int32 [4096], P(('box', 'samp')), may hold values from 0 to 511, as said below
- translators: float32 [64, 2, 2048], P(None, None, 'samp'), may hold values from -0.5 to 0.5
- inter_list: int32 [512, 16], P('box'), may hold values from 0 to 511, as said below
- trans_id: int32 [512, 16], P('box'), may hold values from 0 to 63
Outputs:
- product: float32 [4096, 2, 4, 128], P(('box', 'samp'))
Inputs may be any that keep to these rules, and one draw needn't show every extreme that they name: `neighbours`: row n starts with n itself; its other entries are distinct and lie within 8 boxes of n in cyclic order over all 4096 leaf boxes (the texture is periodic). `leaf_parent_index`: leaf box n belongs to box group g = n // 256 and its parent is one of that group's upper-level boxes g * 32 to g * 32 + 31; every upper-level box has exactly 8 children. `octant`: the 8 children of an upper-level box have 8 distinct octants. `inter_list`: entries of row p are distinct, each equal to p + d modulo 512 with 2 <= |d| <= 32 (the periodic tree's interaction zone). `phases`: each entry has magnitude one: real part squared plus imaginary part squared is 1.
All inputs are finite; a program needn't handle non-finite values.
Results may differ from a plain program's by a relative error of at most 0.0065.
Values may be sent and summed in bfloat16 or wider, within the bound.
A program may use at most 64 MiB of HBM per device.

v0:
```python
import jax
import jax.numpy as jnp
from jax import lax
from jax.sharding import PartitionSpec as P


def with_halo(cells, sides, width):
    for axis, dim in sides:
        count = lax.axis_size(axis)
        head = lax.slice_in_dim(cells, 0, width, axis=dim)
        tail = lax.slice_in_dim(cells, cells.shape[dim] - width, cells.shape[dim], axis=dim)
        cells = jnp.concatenate(
            [
                lax.ppermute(tail, axis, [(i, (i + 1) % count) for i in range(count)]),
                cells,
                lax.ppermute(head, axis, [((i + 1) % count, i) for i in range(count)]),
            ],
            axis=dim,
        )
    return cells


def cmul(ar, ai, br, bi):
    return (ar * br - ai * bi, ar * bi + ai * br)


def on_device(
    xvec,
    near_blocks,
    neighbours,
    lift,
    place,
    interp,
    phases,
    octant,
    leaf_parent_index,
    translators,
    inter_list,
    trans_id,
):
    f32 = jnp.float32
    bf16 = jnp.bfloat16
    finest_precision = lax.Precision.HIGHEST
    boxes = xvec.shape[0]
    nsamp = lax.axis_size("samp")
    nboxaxis = lax.axis_size("box")
    box_index = lax.axis_index("box")
    samp_index = lax.axis_index("samp")
    compute_unit = box_index * nsamp + samp_index
    total = boxes * nsamp * nboxaxis
    reach = boxes // 2
    parents_here = boxes * nsamp // 8
    all_parents = parents_here * nboxaxis
    sample_share = interp.shape[0] // nsamp
    rhs_count = xvec.shape[2]
    widened = with_halo(xvec, ((("box", "samp"), 0),), reach)
    local_index = jnp.mod(neighbours - compute_unit * boxes + reach, total)
    near_x = jnp.take(widened, local_index, axis=0)

    def apply(a, b):
        return jnp.einsum("bkpq,bkrq->brp", a, b, preferred_element_type=f32)

    near_r = apply(near_blocks[:, :, 0], near_x[:, :, 0]) - apply(
        near_blocks[:, :, 1], near_x[:, :, 1]
    )
    near_i = apply(near_blocks[:, :, 0], near_x[:, :, 1]) + apply(
        near_blocks[:, :, 1], near_x[:, :, 0]
    )

    def radiate(a, b):
        return jnp.einsum("bqu,bru->brq", a, b, preferred_element_type=f32)

    pat_r = radiate(lift[:, 0], xvec[:, 0]) - radiate(lift[:, 1], xvec[:, 1])
    pat_i = radiate(lift[:, 0], xvec[:, 1]) + radiate(lift[:, 1], xvec[:, 0])
    pattern = jnp.stack([pat_r, pat_i], 1).astype(bf16)

    def phase_rows(octs):
        indicator_matrix = (octs[:, None] == jnp.arange(8, dtype=jnp.int32)[None, :]).astype(f32)
        return jnp.einsum("ex,xwf->ewf", indicator_matrix, phases, precision=finest_precision)

    def parent_table(pars):
        local = pars - box_index * parents_here
        return local[:, None] == jnp.arange(parents_here, dtype=jnp.int32)[None, :]

    rows_i = interp
    raised_terms = jnp.einsum("sq,bcrq->bcrs", rows_i, pattern, preferred_element_type=f32)
    shift = phase_rows(octant)
    cr, ci = cmul(
        shift[:, 0][:, None, :], shift[:, 1][:, None, :], raised_terms[:, 0], raised_terms[:, 1]
    )
    owner = parent_table(leaf_parent_index).astype(f32)
    sum_r = jnp.einsum("bp,brs->prs", owner, cr, precision=finest_precision)
    sum_i = jnp.einsum("bp,brs->prs", owner, ci, precision=finest_precision)
    term = jnp.stack([sum_r, sum_i], 1)
    term = term.reshape(parents_here, 2, rhs_count, 1 * lax.axis_size("samp"), sample_share)
    upward = lax.psum_scatter(
        jnp.transpose(term, (3, 0, 1, 2, 4)), "samp", scatter_dimension=0, tiled=True
    )[0]
    parent_pat = upward.astype(bf16)
    table_count = translators.shape[0]
    selector_index = (
        trans_id[:, :, None] == jnp.arange(table_count, dtype=jnp.int32)[None, None, :]
    ).astype(f32)
    operator_list = jnp.einsum(
        "yaw,wjt->yajt", selector_index, translators, precision=finest_precision
    )
    bordered = with_halo(parent_pat, (("box", 0),), parents_here)
    window_index = jnp.mod(inter_list - box_index * parents_here + parents_here, all_parents)
    select = (
        window_index[:, :, None] == jnp.arange(3 * parents_here, dtype=jnp.int32)[None, None, :]
    ).astype(bf16)
    fetched = jnp.einsum("pkj,jcrs->pkcrs", select, bordered, preferred_element_type=f32)
    tr_r = operator_list[:, :, 0][:, :, None, :]
    tr_i = operator_list[:, :, 1][:, :, None, :]
    add_r, add_i = cmul(tr_r, tr_i, fetched[:, :, 0], fetched[:, :, 1])
    incoming = jnp.stack([add_r.sum(1), add_i.sum(1)], 1).astype(bf16)
    owner = parent_table(leaf_parent_index).astype(bf16)
    chosen = jnp.einsum(
        "ei,ihfz->ehfz",
        owner,
        lax.all_gather(incoming, "samp", axis=3, tiled=True),
        preferred_element_type=f32,
    )
    shift = phase_rows(octant)
    sr, si = cmul(shift[:, 0][:, None, :], shift[:, 1][:, None, :], chosen[:, 0], chosen[:, 1])
    shifted = jnp.stack([sr, si], 1).astype(bf16)
    rows_i = interp
    field = jnp.einsum("bcrs,sq->bcrq", shifted, rows_i, preferred_element_type=f32)
    field = field.astype(bf16)

    def receive(a, b):
        return jnp.einsum("buq,brq->bru", a, b, preferred_element_type=f32)

    far_r = receive(place[:, 0], field[:, 0]) - receive(place[:, 1], field[:, 1])
    far_i = receive(place[:, 0], field[:, 1]) + receive(place[:, 1], field[:, 0])
    return jnp.stack([near_r + far_r, near_i + far_i], 1)


def solution(mesh):
    in_specs = (
        P(("box", "samp"), None, None, None),
        P(("box", "samp"), None, None, None, None),
        P(("box", "samp"), None),
        P(("box", "samp"), None, None, None),
        P(("box", "samp"), None, None, None),
        P(),
        P(),
        P(("box", "samp")),
        P(("box", "samp")),
        P(None, None, "samp"),
        P("box", None),
        P("box", None),
    )
    out_specs = P(("box", "samp"), None, None, None)
    return jax.shard_map(
        on_device, mesh=mesh, in_specs=in_specs, out_specs=out_specs, check_vma=False
    )
```

profile of v0, /device:TPU:8, one launch (start us, length us, event | category | flops | bytes accessed | tf_op | source)
XLA Modules:
  0.0 224.2 jit_solution(11524168463856257246)
XLA Ops:
  6.5 1.5 fusion.53
  8.0 1.4 fusion.55
  9.5 1.3 fusion.79
  10.8 1.4 fusion.36
  12.2 1.4 fusion.37
  13.7 0.3 fusion.58
  14.2 0.7 convolution_bitcast_fusion
  14.9 0.7 convolution_bitcast_fusion.1
  15.8 115.4 %all-reduce.2 = bf16[16,32,2,4,128]{4,1,0,3,2:T(8,128)(2,1)} all-reduce(f32[16,32,2,4,128]{4,1,0,3,2:T(8,128)S(1)} %maximum_bitcast_fusion), channel_id=2, replica_groups=mesh['box'=16,'samp'=16] {'samp'}, use_global_device_ids=true, to_apply=%region_0.1.clone | all-reduce | flops 524288 | bytes 3145728
  131.2 0.6 dynamic-slice
  131.8 1.5 fusion.83
  133.3 1.7 collective-permute-start.3
  135.1 2.6 %collective-permute-start = (bf16[8,2,4,128]{3,2,1,0:T(4,128)(2,1)S(1)}, bf16[8,2,4,128]{3,2,1,0:T(4,128)(2,1)S(1)}, u32[]{:S(2)}, u32[]{:S(2)}) collective-permute-start(bf16[8,2,4,128]{3,2,1,0:T(4,128)(2,1)S(1)} %get-tuple-element.19), channel_id=1, source_target_pairs={{0,1},{1,2},{2,3},{3,4},{4,5},{5,6},{6,7},{7,8},{8,9},{9,10},{10,1... | collective-permute-start | bytes 49160 | tf_op jit(solution)/shard_map/ppermute | solution.py:14
  137.7 3.7 %collective-permute-start.1 = (bf16[8,2,4,128]{3,2,1,0:T(4,128)(2,1)S(1)}, bf16[8,2,4,128]{3,2,1,0:T(4,128)(2,1)S(1)}, u32[]{:S(2)}, u32[]{:S(2)}) collective-permute-start(bf16[8,2,4,128]{3,2,1,0:T(4,128)(2,1)S(1)} %get-tuple-element.20), channel_id=1, source_target_pairs={{1,0},{2,1},{3,2},{4,3},{5,4},{6,5},{7,6},{8,7},{9,8},{10,9},{11,1... | collective-permute-start | bytes 49160 | tf_op jit(solution)/shard_map/ppermute | solution.py:16
  141.5 0.4 fusion.69
  142.1 0.5 fusion.72
  142.6 0.7 subtract_reduce_fusion
  143.3 0.6 pad_maximum_fusion.1
  144.3 0.8 gather_fusion
  145.2 0.2 broadcast_select_fusion
  145.4 3.4 %fusion.12 = f32[16,4,128]{2,1,0:T(4,128)S(1)} fusion(bf16[16,8,2,128,128]{4,3,2,1,0:T(8,128)(2,1)} %param.13, bf16[16,8,2,4,128]{4,3,1,0,2:T(4,128)(2,1)S(1)} %broadcast_select_fusion), kind=kOutput, calls=%fused_computation.17 | convolution fusion | flops 16777216 | bytes 4358144 | tf_op jit(solution)/shard_map/bkpq,bkrq->brp/dot_general | solution.py:61
  148.8 3.5 %fusion.15 = f32[16,4,128]{2,1,0:T(4,128)S(1)} fusion(bf16[16,8,2,128,128]{4,3,2,1,0:T(8,128)(2,1)} %param.13, bf16[16,8,2,4,128]{4,3,1,0,2:T(4,128)(2,1)S(1)} %broadcast_select_fusion), kind=kOutput, calls=%fused_computation.18 | convolution fusion | flops 16777216 | bytes 4358144 | tf_op jit(solution)/shard_map/bkpq,bkrq->brp/dot_general | solution.py:61
  152.3 3.4 %fusion.31 = f32[16,4,128]{2,1,0:T(4,128)S(1)} fusion(f32[16,4,128]{2,1,0:T(4,128)S(1)} %fusion.12, bf16[16,8,2,128,128]{4,3,2,1,0:T(8,128)(2,1)} %param.13, bf16[16,8,2,4,128]{4,3,1,0,2:T(4,128)(2,1)S(1)} %broadcast_select_fusion), kind=kOutput, calls=%fused_computation.30 | convolution fusion | flops 16785408 | bytes 4390912 | tf_op jit(solution)/shard_map/bkpq,bkrq->brp/dot_general | solution.py:61
  155.7 3.5 %fusion.28 = f32[16,4,128]{2,1,0:T(4,128)S(1)} fusion(f32[16,4,128]{2,1,0:T(4,128)S(1)} %fusion.15, bf16[16,8,2,128,128]{4,3,2,1,0:T(8,128)(2,1)} %param.13, bf16[16,8,2,4,128]{4,3,1,0,2:T(4,128)(2,1)S(1)} %broadcast_select_fusion), kind=kOutput, calls=%fused_computation.29 | convolution fusion | flops 16785408 | bytes 4390912 | tf_op jit(solution)/shard_map/bkpq,bkrq->brp/dot_general | solution.py:61
  159.2 53.9 %all-gather.2.cloned.1.call-done = bf16[32,2,4,2048]{3,0,2,1:T(8,128)(2,1)} async-done(((bf16[32,2,4,128]{3,0,2,1:T(8,128)(2,1)}), bf16[32,2,4,2048]{3,0,2,1:T(8,128)(2,1)}) %all-gather.2.cloned.1.call-update) | async-done | bytes 1048592 | tf_op jit(solution)/shard_map/all_gather | solution.py:121
  213.1 1.6 fusion.103
  214.8 0.3 convolution_convert_fusion
  215.1 0.4 fusion.49
  215.5 0.4 fusion.47
  215.9 0.4 fusion.27
  216.3 0.4 fusion.25
  216.7 0.6 copy.87
  (46 shorter events, 1.3 us)
Async XLA Ops:
  6.5 7.2 %copy-start = (bf16[2048,128]{1,0:T(8,128)(2,1)S(1)}, bf16[2048,128]{1,0:T(8,128)(2,1)}, u32[]{:S(2)}) copy-start(bf16[2048,128]{1,0:T(8,128)(2,1)} %param.17) | copy-start | bytes 1572868
  6.5 7.5 %copy-start.7 = (s32[16]{0:T(128)S(1)}, s32[16]{0:T(128)}, u32[]{:S(2)}) copy-start(s32[16]{0:T(128)} %param.20) | copy-start | bytes 196
  6.5 206.5 %all-gather.2.cloned.1.call-start = ((), (), s32[]{:S(2)}) async-start(), calls=%async_computation | async-start | bytes 1114112 | tf_op jit(solution)/shard_map/all_gather | solution.py:121
  14.9 116.4 %copy-start.8 = (u32[256]{0:T(256)S(1)}, u32[256]{0:T(256)}, u32[]{:S(2)}) copy-start(u32[256]{0:T(256)} %constant.68) | copy-start | bytes 3076
  14.9 120.2 %copy-start.2 = (bf16[16,2,4,128]{3,2,1,0:T(4,128)(2,1)S(1)}, bf16[16,2,4,128]{3,2,1,0:T(4,128)(2,1)}, u32[]{:S(2)}) copy-start(bf16[16,2,4,128]{3,2,1,0:T(4,128)(2,1)} %param.12) | copy-start | bytes 98308
  14.9 126.5 %copy-start.4 = (s32[32,16]{0,1:T(8,128)S(1)}, s32[32,16]{0,1:T(8,128)}, u32[]{:S(2)}) copy-start(s32[32,16]{0,1:T(8,128)} %param.23) | copy-start | bytes 6148
  14.9 126.6 %copy-start.3 = (f32[64,2,128]{2,1,0:T(2,128)S(1)}, f32[64,2,128]{2,1,0:T(2,128)}, u32[]{:S(2)}) copy-start(f32[64,2,128]{2,1,0:T(2,128)} %param.21) | copy-start | bytes 196612
  15.6 126.4 %copy-start.5 = (s32[32,16]{0,1:T(8,128)S(1)}, s32[32,16]{0,1:T(8,128)}, u32[]{:S(2)}) copy-start(s32[32,16]{0,1:T(8,128)} %param.22) | copy-start | bytes 6148
  131.2 12.7 %copy-start.6 = (s32[16,8]{0,1:T(8,128)S(1)}, s32[16,8]{0,1:T(8,128)}, u32[]{:S(2)}) copy-start(s32[16,8]{0,1:T(8,128)} %param.14) | copy-start | bytes 1540
  133.3 8.8 %collective-permute-start.2 = (bf16[32,2,4,128]{3,0,2,1:T(8,128)(2,1)S(1)}, bf16[32,2,4,128]{3,0,2,1:T(8,128)(2,1)S(1)}, u32[]{:S(2)}, u32[]{:S(2)}) collective-permute-start(bf16[32,2,4,128]{3,0,2,1:T(8,128)(2,1)S(1)} %fusion.83), channel_id=1, source_target_pairs={{0,16},{16,32},{32,48},{48,64},{64,80},{80,96},{96,112},{112,128},... | collective-permute-start | bytes 196616 | tf_op jit(solution)/shard_map/ppermute | solution.py:14
  133.3 8.8 %collective-permute-start.3 = (bf16[32,2,4,128]{3,0,2,1:T(8,128)(2,1)S(1)}, bf16[32,2,4,128]{3,0,2,1:T(8,128)(2,1)S(1)}, u32[]{:S(2)}, u32[]{:S(2)}) collective-permute-start(bf16[32,2,4,128]{3,0,2,1:T(8,128)(2,1)S(1)} %fusion.83), channel_id=1, source_target_pairs={{16,0},{32,16},{48,32},{64,48},{80,64},{96,80},{112,96},{128,112},... | collective-permute-start | bytes 196616 | tf_op jit(solution)/shard_map/ppermute | solution.py:16
  135.1 9.2 %collective-permute-start = (bf16[8,2,4,128]{3,2,1,0:T(4,128)(2,1)S(1)}, bf16[8,2,4,128]{3,2,1,0:T(4,128)(2,1)S(1)}, u32[]{:S(2)}, u32[]{:S(2)}) collective-permute-start(bf16[8,2,4,128]{3,2,1,0:T(4,128)(2,1)S(1)} %get-tuple-element.19), channel_id=1, source_target_pairs={{0,1},{1,2},{2,3},{3,4},{4,5},{5,6},{6,7},{7,8},{8,9},{9,10},{10,1... | collective-permute-start | bytes 49160 | tf_op jit(solution)/shard_map/ppermute | solution.py:14
  137.7 6.5 %collective-permute-start.1 = (bf16[8,2,4,128]{3,2,1,0:T(4,128)(2,1)S(1)}, bf16[8,2,4,128]{3,2,1,0:T(4,128)(2,1)S(1)}, u32[]{:S(2)}, u32[]{:S(2)}) collective-permute-start(bf16[8,2,4,128]{3,2,1,0:T(4,128)(2,1)S(1)} %get-tuple-element.20), channel_id=1, source_target_pairs={{1,0},{2,1},{3,2},{4,3},{5,4},{6,5},{7,6},{8,7},{9,8},{10,9},{11,1... | collective-permute-start | bytes 49160 | tf_op jit(solution)/shard_map/ppermute | solution.py:16
  155.7 59.4 %copy-start.1 = (bf16[16,2,128,128]{3,2,1,0:T(8,128)(2,1)S(1)}, bf16[16,2,128,128]{3,2,1,0:T(8,128)(2,1)}, u32[]{:S(2)}) copy-start(bf16[16,2,128,128]{3,2,1,0:T(8,128)(2,1)} %param.16) | copy-start | bytes 3145732
Sparse Core Ops, SparseCore 0:
  144.0 69.0 all-gather.1
where the time goes:
time: 225 us; the launch traced here: 224 us
  blocking collectives  115 us (51%)
  waiting for transfers between devices  53.9 us (24%)
  matrix products  26.8 us (12%)
  between operations  13.7 us (6%)
  starting transfers between devices  8.09 us (4%)
  local copies, waits for them, and re-layouts  4.17 us (2%)
    unnamed x1, blocking collectives  115 us
    all_gather x1, waiting for transfers between devices, on_device(): lax.all_gather(incoming, 'samp', axis=3, tiled=True)  53.9 us
    dot_general x4, matrix products, apply(): return jnp.einsum('bkpq,bkrq->brp', a, b, preferred_element_type=f32)  13.8 us
    dot_general x4, matrix products, radiate(): return jnp.einsum('bqu,bru->brq', a, b, preferred_element_type=f32)  5.78 us
    ppermute x2, starting transfers between devices, with_halo(): lax.ppermute(head, axis, [((i + 1) % count, i) for i in range(count)])  5.47 us
  transfers between devices with their start and end apart: 5, of which 1 were waited for; matrix products, arithmetic and copies ran while one was open for 8% of the time, Pallas kernels for 0%

commit v1 on v0

--- a/solution.py
+++ b/solution.py
@@ -118,7 +118,12 @@
     chosen = jnp.einsum(
         "ei,ihfz->ehfz",
         owner,
-        lax.all_gather(incoming, "samp", axis=3, tiled=True),
+        jnp.concatenate(
+            lax.all_to_all(
+                jnp.stack([incoming for _ in range(lax.axis_size("samp"))]), "samp", 0, 0
+            ),
+            3,
+        ),
         preferred_element_type=f32,
     )
     shift = phase_rows(octant)

time: 225 us -> 174 us (0.77)
  waiting for transfers between devices: 53.9 us -> 13.3 us
  between operations: 13.7 us -> 0.3 us
  starting transfers between devices: 8.09 us -> 11.9 us
    all_gather x1 -> x0, waiting for transfers between devices: 53.9 us -> none  [on_device(): lax.all_gather(incoming, 'samp', axis=3, tiled=True)]
    all_to_all x0 -> x1, waiting for transfers between devices: none -> 13.3 us  [on_device(): lax.all_to_all(jnp.stack([incoming for _ in range(lax.axis_size('samp'))]...]
    all_to_all x0 -> x1, starting transfers between devices: none -> 3.83 us  [on_device(): lax.all_to_all(jnp.stack([incoming for _ in range(lax.axis_size('samp'))]...]
  transfers between devices with their start and end apart: 5 -> 5, of which waited for: 1 -> 1; matrix products, arithmetic and copies ran while one was open for 8% -> 11% of each run, Pallas kernels for 0% -> 0%
where the time goes in v1:
time: 174 us; the launch traced here: 172 us
  blocking collectives  114 us (66%)
  matrix products  25.5 us (15%)
  waiting for transfers between devices  13.3 us (8%)
  starting transfers between devices  11.9 us (7%)
  local copies, waits for them, and re-layouts  5.39 us (3%)
    unnamed x1, blocking collectives  114 us
    dot_general x4, matrix products, apply(): return jnp.einsum('bkpq,bkrq->brp', a, b, preferred_element_type=f32)  13.7 us
    all_to_all x1, waiting for transfers between devices, on_device(): lax.all_to_all(jnp.stack([incoming for _ in range(lax.axis_size('samp'))]...  13.3 us
    ppermute x2, starting transfers between devices, with_halo(): lax.ppermute(head, axis, [((i + 1) % count, i) for i in range(count)])  6.46 us
    dot_general x4, matrix products, radiate(): return jnp.einsum('bqu,bru->brq', a, b, preferred_element_type=f32)  5.79 us
    all_to_all x1, starting transfers between devices, on_device(): lax.all_to_all(jnp.stack([incoming for _ in range(lax.axis_size('samp'))]...  3.83 us
  transfers between devices with their start and end apart: 5, of which 1 were waited for; matrix products, arithmetic and copies ran while one was open for 11% of the time, Pallas kernels for 0%

profile of v1, /device:TPU:8, one launch (start us, length us, event | category | flops | bytes accessed | tf_op | source)
XLA Modules:
  0.0 172.1 jit_solution(14544874465984397714)
XLA Ops:
  0.0 1.5 fusion.56
  1.5 1.4 fusion.58
  2.9 1.3 fusion.82
  4.2 1.4 fusion.36
  5.6 1.4 fusion.37
  7.2 0.3 fusion.61
  7.6 0.7 convolution_bitcast_fusion
  8.4 0.7 convolution_bitcast_fusion.1
  9.3 114.1 %all-reduce.2 = bf16[16,32,2,4,128]{4,1,0,3,2:T(8,128)(2,1)} all-reduce(f32[16,32,2,4,128]{4,1,0,3,2:T(8,128)S(1)} %maximum_bitcast_fusion), channel_id=2, replica_groups=mesh['box'=16,'samp'=16] {'samp'}, use_global_device_ids=true, to_apply=%region_0.1.clone | all-reduce | flops 524288 | bytes 3145728
  123.4 0.6 dynamic-slice
  124.0 1.5 fusion.86
  125.5 1.7 %collective-permute-start.3 = (bf16[32,2,4,128]{3,0,2,1:T(8,128)(2,1)S(1)}, bf16[32,2,4,128]{3,0,2,1:T(8,128)(2,1)S(1)}, u32[]{:S(2)}, u32[]{:S(2)}) collective-permute-start(bf16[32,2,4,128]{3,0,2,1:T(8,128)(2,1)S(1)} %fusion.86), channel_id=1, source_target_pairs={{16,0},{32,16},{48,32},{64,48},{80,64},{96,80},{112,96},{128,112},... | collective-permute-start | bytes 196616 | tf_op jit(solution)/shard_map/ppermute | solution.py:16
  127.2 1.6 collective-permute-start
  128.9 4.7 %collective-permute-start.1 = (bf16[8,2,4,128]{3,2,1,0:T(4,128)(2,1)S(1)}, bf16[8,2,4,128]{3,2,1,0:T(4,128)(2,1)S(1)}, u32[]{:S(2)}, u32[]{:S(2)}) collective-permute-start(bf16[8,2,4,128]{3,2,1,0:T(4,128)(2,1)S(1)} %get-tuple-element.20), channel_id=1, source_target_pairs={{1,0},{2,1},{3,2},{4,3},{5,4},{6,5},{7,6},{8,7},{9,8},{10,9},{11,1... | collective-permute-start | bytes 49160 | tf_op jit(solution)/shard_map/ppermute | solution.py:16
  133.7 0.4 fusion.72
  134.3 0.5 fusion.75
  134.7 0.7 subtract_reduce_fusion
  135.5 1.2 stack.67
  136.7 3.8 %all-to-all-start = ((bf16[16,32,2,4,128]{4,1,3,2,0:T(8,128)(2,1)}), bf16[16,32,2,4,128]{4,1,3,2,0:T(8,128)(2,1)S(1)}, u32[]{:S(2)}, u32[]{:S(2)}) async-start(bf16[16,32,2,4,128]{4,1,3,2,0:T(8,128)(2,1)} %stack.67), calls=%async_computation | async-start | bytes 2097152 | tf_op jit(solution)/shard_map/all_to_all | solution.py:122
  140.9 0.8 gather_fusion
  142.1 3.4 %fusion.12 = f32[16,4,128]{2,1,0:T(4,128)S(1)} fusion(bf16[16,8,2,128,128]{4,3,2,1,0:T(8,128)(2,1)} %param.13, bf16[16,8,2,4,128]{4,3,1,0,2:T(4,128)(2,1)S(1)} %broadcast_select_fusion), kind=kOutput, calls=%fused_computation.17 | convolution fusion | flops 16777216 | bytes 4358144 | tf_op jit(solution)/shard_map/bkpq,bkrq->brp/dot_general | solution.py:61
  145.5 3.4 %fusion.15 = f32[16,4,128]{2,1,0:T(4,128)S(1)} fusion(bf16[16,8,2,128,128]{4,3,2,1,0:T(8,128)(2,1)} %param.13, bf16[16,8,2,4,128]{4,3,1,0,2:T(4,128)(2,1)S(1)} %broadcast_select_fusion), kind=kOutput, calls=%fused_computation.18 | convolution fusion | flops 16777216 | bytes 4358144 | tf_op jit(solution)/shard_map/bkpq,bkrq->brp/dot_general | solution.py:61
  148.9 3.4 %fusion.31 = f32[16,4,128]{2,1,0:T(4,128)S(1)} fusion(f32[16,4,128]{2,1,0:T(4,128)S(1)} %fusion.12, bf16[16,8,2,128,128]{4,3,2,1,0:T(8,128)(2,1)} %param.13, bf16[16,8,2,4,128]{4,3,1,0,2:T(4,128)(2,1)S(1)} %broadcast_select_fusion), kind=kOutput, calls=%fused_computation.30 | convolution fusion | flops 16785408 | bytes 4390912 | tf_op jit(solution)/shard_map/bkpq,bkrq->brp/dot_general | solution.py:61
  152.3 3.5 %fusion.28 = f32[16,4,128]{2,1,0:T(4,128)S(1)} fusion(f32[16,4,128]{2,1,0:T(4,128)S(1)} %fusion.15, bf16[16,8,2,128,128]{4,3,2,1,0:T(8,128)(2,1)} %param.13, bf16[16,8,2,4,128]{4,3,1,0,2:T(4,128)(2,1)S(1)} %broadcast_select_fusion), kind=kOutput, calls=%fused_computation.29 | convolution fusion | flops 16785408 | bytes 4390912 | tf_op jit(solution)/shard_map/bkpq,bkrq->brp/dot_general | solution.py:61
  155.8 13.3 %all-to-all-done = bf16[16,32,2,4,128]{4,1,3,2,0:T(8,128)(2,1)S(1)} async-done(((bf16[16,32,2,4,128]{4,1,3,2,0:T(8,128)(2,1)}), bf16[16,32,2,4,128]{4,1,3,2,0:T(8,128)(2,1)S(1)}, u32[]{:S(2)}, u32[]{:S(2)}) %all-to-all-start) | async-done | bytes 1048608 | tf_op jit(solution)/shard_map/all_to_all | solution.py:122
  169.1 0.3 fusion.38
  169.6 0.3 convolution_convert_fusion
  169.9 0.4 fusion.52
  170.3 0.4 fusion.50
  170.7 0.4 fusion.27
  171.1 0.4 fusion.25
  171.5 0.6 copy.87
  (46 shorter events, 1.6 us)
Async XLA Ops:
  0.0 7.1 %copy-start = (bf16[2048,128]{1,0:T(8,128)(2,1)S(1)}, bf16[2048,128]{1,0:T(8,128)(2,1)}, u32[]{:S(2)}) copy-start(bf16[2048,128]{1,0:T(8,128)(2,1)} %param.17) | copy-start | bytes 1572868
  0.0 7.5 %copy-start.7 = (s32[16]{0:T(128)S(1)}, s32[16]{0:T(128)}, u32[]{:S(2)}) copy-start(s32[16]{0:T(128)} %param.20) | copy-start | bytes 196
  8.3 115.1 %copy-start.8 = (u32[256]{0:T(256)S(1)}, u32[256]{0:T(256)}, u32[]{:S(2)}) copy-start(u32[256]{0:T(256)} %constant.68) | copy-start | bytes 3076
  8.3 118.9 %copy-start.2 = (bf16[16,2,4,128]{3,2,1,0:T(4,128)(2,1)S(1)}, bf16[16,2,4,128]{3,2,1,0:T(4,128)(2,1)}, u32[]{:S(2)}) copy-start(bf16[16,2,4,128]{3,2,1,0:T(4,128)(2,1)} %param.12) | copy-start | bytes 98308
  8.3 125.2 %copy-start.4 = (s32[32,16]{0,1:T(8,128)S(1)}, s32[32,16]{0,1:T(8,128)}, u32[]{:S(2)}) copy-start(s32[32,16]{0,1:T(8,128)} %param.23) | copy-start | bytes 6148
  8.4 125.3 %copy-start.3 = (f32[64,2,128]{2,1,0:T(2,128)S(1)}, f32[64,2,128]{2,1,0:T(2,128)}, u32[]{:S(2)}) copy-start(f32[64,2,128]{2,1,0:T(2,128)} %param.21) | copy-start | bytes 196612
  9.1 125.1 %copy-start.5 = (s32[32,16]{0,1:T(8,128)S(1)}, s32[32,16]{0,1:T(8,128)}, u32[]{:S(2)}) copy-start(s32[32,16]{0,1:T(8,128)} %param.22) | copy-start | bytes 6148
  125.5 8.8 %collective-permute-start.2 = (bf16[32,2,4,128]{3,0,2,1:T(8,128)(2,1)S(1)}, bf16[32,2,4,128]{3,0,2,1:T(8,128)(2,1)S(1)}, u32[]{:S(2)}, u32[]{:S(2)}) collective-permute-start(bf16[32,2,4,128]{3,0,2,1:T(8,128)(2,1)S(1)} %fusion.86), channel_id=1, source_target_pairs={{0,16},{16,32},{32,48},{48,64},{64,80},{80,96},{96,112},{112,128},... | collective-permute-start | bytes 196616 | tf_op jit(solution)/shard_map/ppermute | solution.py:14
  125.5 8.8 %collective-permute-start.3 = (bf16[32,2,4,128]{3,0,2,1:T(8,128)(2,1)S(1)}, bf16[32,2,4,128]{3,0,2,1:T(8,128)(2,1)S(1)}, u32[]{:S(2)}, u32[]{:S(2)}) collective-permute-start(bf16[32,2,4,128]{3,0,2,1:T(8,128)(2,1)S(1)} %fusion.86), channel_id=1, source_target_pairs={{16,0},{32,16},{48,32},{64,48},{80,64},{96,80},{112,96},{128,112},... | collective-permute-start | bytes 196616 | tf_op jit(solution)/shard_map/ppermute | solution.py:16
  127.2 13.6 %collective-permute-start = (bf16[8,2,4,128]{3,2,1,0:T(4,128)(2,1)S(1)}, bf16[8,2,4,128]{3,2,1,0:T(4,128)(2,1)S(1)}, u32[]{:S(2)}, u32[]{:S(2)}) collective-permute-start(bf16[8,2,4,128]{3,2,1,0:T(4,128)(2,1)S(1)} %get-tuple-element.19), channel_id=1, source_target_pairs={{0,1},{1,2},{2,3},{3,4},{4,5},{5,6},{6,7},{7,8},{8,9},{9,10},{10,1... | collective-permute-start | bytes 49160 | tf_op jit(solution)/shard_map/ppermute | solution.py:14
  128.9 12.0 %collective-permute-start.1 = (bf16[8,2,4,128]{3,2,1,0:T(4,128)(2,1)S(1)}, bf16[8,2,4,128]{3,2,1,0:T(4,128)(2,1)S(1)}, u32[]{:S(2)}, u32[]{:S(2)}) collective-permute-start(bf16[8,2,4,128]{3,2,1,0:T(4,128)(2,1)S(1)} %get-tuple-element.20), channel_id=1, source_target_pairs={{1,0},{2,1},{3,2},{4,3},{5,4},{6,5},{7,6},{8,7},{9,8},{10,9},{11,1... | collective-permute-start | bytes 49160 | tf_op jit(solution)/shard_map/ppermute | solution.py:16
  134.2 6.3 %copy-start.6 = (s32[16,8]{0,1:T(8,128)S(1)}, s32[16,8]{0,1:T(8,128)}, u32[]{:S(2)}) copy-start(s32[16,8]{0,1:T(8,128)} %param.14) | copy-start | bytes 1540
  136.7 32.4 %all-to-all-start = ((bf16[16,32,2,4,128]{4,1,3,2,0:T(8,128)(2,1)}), bf16[16,32,2,4,128]{4,1,3,2,0:T(8,128)(2,1)S(1)}, u32[]{:S(2)}, u32[]{:S(2)}) async-start(bf16[16,32,2,4,128]{4,1,3,2,0:T(8,128)(2,1)} %stack.67), calls=%async_computation | async-start | bytes 2097152 | tf_op jit(solution)/shard_map/all_to_all | solution.py:122
  152.3 17.6 %copy-start.1 = (bf16[16,2,128,128]{3,2,1,0:T(8,128)(2,1)S(1)}, bf16[16,2,128,128]{3,2,1,0:T(8,128)(2,1)}, u32[]{:S(2)}) copy-start(bf16[16,2,128,128]{3,2,1,0:T(8,128)(2,1)} %param.16) | copy-start | bytes 3145732
